TPU v7x, 512 devices: a whole 4x8x8 slice. The times are simulated.
512 devices in a mesh: grp: 4 (over x), dev: 128 (over z, y, core).
Axes of the slice: x: 4, y: 8, z: 8, core: 2. Of those that a mesh axis runs over, the one named last changes fastest.
Arguments:
- blocks: bfloat16 [4096, 64, 4096], P(('grp', 'dev')), may hold values from -6 to 6
- coords: int32 [3, 4096], P(None, ('grp', 'dev')), may hold values from 0 to 255, as said below
- counts: int32 [512], P(('grp', 'dev')), may hold values from 1 to 8, as said below
- row_place: int32 [256], replicated, may hold values from 0 to 255, as said below
- factor_one: bfloat16 [256, 4096], P('dev'), may hold values from -0.75 to 0.75
- factor_two: bfloat16 [256, 4096], P('dev'), may hold values from -0.75 to 0.75
- factor_three: bfloat16 [256, 4096], P('dev'), may hold values from -0.75 to 0.75
Outputs:
- new_rows: float32 [256, 4096], P('dev')
- gram: float32 [64, 64], replicated
Inputs may be any that keep to these rules, and one draw needn't show every extreme that they name: `coords`: every mode-1 id of a slot on the device with dev index d has its row-block position in [d * 2, (d + 1) * 2); on one device, the row-block positions of the mode-2 ids of its 8 slots lie in pairwise different ranges [e * 2, (e + 1) * 2), and so do those of the mode-3 ids. `counts`: some device has all 8 slots live. `row_place`: A permutation of 0 to 255.
All inputs are finite; a program needn't handle non-finite values.
Results may differ from a plain program's by a relative error of at most 0.0056.
Values may be sent and summed in bfloat16 or wider, within the bound.
A program may use at most 128 MiB of HBM per device.

v0:
```python
import jax
import jax.numpy as jnp
from jax import lax
from jax.sharding import PartitionSpec as P


def look_place(ids, row_place):
    table = jnp.arange(row_place.shape[0])
    hits = ids[:, None] == table[None, :]
    return jnp.sum(jnp.where(hits, row_place[None, :], 0), axis=1)


def body(blocks, coords, counts, row_place, factor_one, factor_two, factor_three):
    slot_count = blocks.shape[0]
    edge = blocks.shape[1]
    rank_width = factor_one.shape[1] // edge
    row_blocks = factor_one.shape[0]
    live = (jnp.arange(slot_count) < counts[0]).astype(jnp.float32)
    pos_one = look_place(coords[0], row_place)
    pos_two = look_place(coords[1], row_place)
    pos_three = look_place(coords[2], row_place)
    local_one = pos_one % row_blocks
    pieces = (
        lax.all_gather(factor_two, "dev", axis=0, tiled=True),
        lax.all_gather(factor_three, "dev", axis=0, tiled=True),
    )
    taken = pieces[0].shape[0]
    offsets = jnp.arange(taken)
    pick_two = (pos_two[:, None] == offsets[None, :]).astype(jnp.bfloat16)
    pick_three = (pos_three[:, None] == offsets[None, :]).astype(jnp.bfloat16)
    chosen_two = jnp.dot(pick_two, pieces[0], preferred_element_type=jnp.float32)
    chosen_three = jnp.dot(pick_three, pieces[1], preferred_element_type=jnp.float32)
    upper = chosen_two.astype(jnp.bfloat16).reshape(slot_count, edge, rank_width)
    lower = chosen_three.astype(jnp.bfloat16).reshape(slot_count, edge, rank_width)
    tensor_rows = blocks.reshape(slot_count, edge * edge, edge)
    first = jnp.einsum(
        "bmk,bks->bms", tensor_rows, lower, preferred_element_type=jnp.float32
    ).astype(jnp.bfloat16)
    first = first.reshape(slot_count, edge, edge, rank_width)
    contrib = jnp.einsum("bajs,bjr->bars", first, upper, preferred_element_type=jnp.float32)
    contrib = contrib.reshape(slot_count, edge, rank_width * rank_width)
    owners = jnp.arange(row_blocks)
    assign = (local_one[:, None] == owners[None, :]).astype(jnp.float32) * live[:, None]
    panels = jnp.einsum("bl,bam->lam", assign, contrib, precision=lax.Precision.HIGHEST)
    panels = panels.reshape(row_blocks * edge, rank_width * rank_width)
    old_rows = factor_one.reshape(row_blocks * edge, rank_width)
    summed = lax.psum(panels, "grp")
    panel_b = summed.astype(jnp.bfloat16)
    proj_terms = jnp.dot(panel_b.T, old_rows, preferred_element_type=jnp.float32)
    proj = lax.psum(proj_terms, "dev").astype(jnp.bfloat16)
    rows = jnp.dot(panel_b, proj, preferred_element_type=jnp.float32)
    gram_local = jnp.dot(
        rows.T, rows, precision=lax.Precision.HIGHEST, preferred_element_type=jnp.float32
    )
    gmat = lax.psum(gram_local, "dev")
    trace_value = jnp.trace(gmat)
    rows_total = row_blocks * edge * lax.axis_size("dev")
    new_rows = (rows * lax.rsqrt(trace_value / (rows_total * rank_width))).reshape(
        row_blocks, edge * rank_width
    )
    gram = gmat * (rank_width / trace_value)
    return (new_rows, gram)


def solution(mesh):
    placed = (
        P(("grp", "dev"), None, None),
        P(None, ("grp", "dev")),
        P(("grp", "dev")),
        P(),
        P("dev", None),
        P("dev", None),
        P("dev", None),
    )
    return jax.shard_map(
        body, mesh=mesh, in_specs=placed, out_specs=(P("dev", None), P()), check_vma=False
    )
```

profile of v0, /device:TPU:4, one launch (start us, length us, event | category | flops | bytes accessed | tf_op | source)
XLA Modules:
  0.0 1270.0 jit_solution(4635308471587969259)
XLA Ops:
  7.2 0.0 copy-start
  7.2 0.0 all-gather.7.cloned.1.call-start
  7.2 0.7 all-gather.7.cloned.1.call-update
  7.9 0.0 all-gather.5.cloned.1.call-start
  8.0 0.7 all-gather.5.cloned.1.call-update
  8.7 12.6 reshape.54
  21.9 0.1 reshape.58
  22.1 0.2 select_reduce_fusion.3
  22.3 76.6 %all-gather.7.cloned.1.call-done = bf16[128,2,4096]{2,1,0:T(2,128)(2,1)} async-done(((bf16[1,2,4096]{2,1,0:T(2,128)(2,1)}), bf16[128,2,4096]{2,1,0:T(2,128)(2,1)}) %all-gather.7.cloned.1.call-update) | async-done | bytes 2097168 | tf_op jit(solution)/shard_map/all_gather | solution.py:25
  98.9 2.7 reshape.63
  101.6 0.4 convolution_convert_fusion.1
  102.0 0.2 reshape.53
  102.2 8.4 fusion.2
  110.7 8.4 copy.40
  119.0 62.9 %all-gather.5.cloned.1.call-done = bf16[128,2,4096]{2,1,0:T(2,128)(2,1)} async-done(((bf16[1,2,4096]{2,1,0:T(2,128)(2,1)}), bf16[128,2,4096]{2,1,0:T(2,128)(2,1)}) %all-gather.5.cloned.1.call-update) | async-done | bytes 2097168 | tf_op jit(solution)/shard_map/all_gather | solution.py:24
  181.9 2.7 reshape.61
  184.7 0.4 convolution_convert_fusion.2
  185.1 0.2 reshape.52
  185.3 11.5 convolution_bitcast_fusion
  196.8 14.8 %reshape.56 = f32[8,64,4096]{2,1,0:T(8,128)} reshape(f32[8,64,64,64]{3,2,1,0:T(8,128)} %convolution_bitcast_fusion) | data formatting | bytes 16777216 | tf_op jit(solution)/shard_map/reshape | solution.py:41
  211.5 15.3 %fusion = f32[2,64,4096]{2,0,1:T(2,128)S(1)} fusion(f32[8,64,4096]{2,1,0:T(8,128)} %reshape.56, f32[8]{0:T(128)S(1)} %compare_convert_fusion, s32[8]{0:T(128)S(1)} %and_select_fusion), kind=kOutput, calls=%fused_computation.1 | convolution fusion | flops 50331680 | bytes 10485824 | tf_op jit(solution)/shard_map/bl,bam->lam/dot_general | solution.py:44
  226.8 1.2 copy.33
  228.1 42.2 %all-reduce.2 = bf16[128,4096]{1,0:T(8,128)(2,1)S(1)} all-reduce(f32[128,4096]{1,0:T(8,128)S(1)} %bitcast.38), channel_id=1, replica_groups=mesh['grp'=4,'dev'=128] {'grp'}, use_global_device_ids=true, to_apply=%region_3.4 | all-reduce | flops 524288 | bytes 3145728 | tf_op jit(solution)/shard_map/psum | solution.py:47
  270.2 0.3 fusion.21
  270.6 497.6 %all-reduce.3 = bf16[4096,64]{0,1:T(8,128)(2,1)S(1)} all-reduce(f32[4096,64]{0,1:T(8,128)S(1)} %fusion.21), channel_id=1, replica_groups=mesh['grp'=4,'dev'=128] {'dev'}, use_global_device_ids=true, to_apply=%region_4.5 | all-reduce | flops 262144 | bytes 1572864 | tf_op jit(solution)/shard_map/psum | solution.py:50
  768.2 0.5 fusion.20
  768.7 0.2 fusion.19
  768.9 490.9 %psum.23 = f32[64,64]{1,0:T(8,128)S(1)} all-reduce(f32[64,64]{1,0:T(8,128)S(1)} %fusion.19), channel_id=1, replica_groups=mesh['grp'=4,'dev'=128] {'dev'}, use_global_device_ids=true, to_apply=%region_5.6 | all-reduce | flops 4096 | bytes 32768 | tf_op jit(solution)/shard_map/psum | solution.py:55
  1259.7 0.6 select_reduce_fusion
  1261.0 0.6 broadcast_multiply_fusion
  1262.4 0.1 copy.34
  1262.4 0.7 reshape.59
  (9 shorter events, 0.0 us)
Async XLA Ops:
  7.2 14.7 %copy-start = (bf16[2,4096]{1,0:T(2,128)(2,1)S(1)}, bf16[2,4096]{1,0:T(2,128)(2,1)}, u32[]{:S(2)}) copy-start(bf16[2,4096]{1,0:T(2,128)(2,1)} %param.11) | copy-start | bytes 49156
  7.2 14.8 %copy-start.1 = (s32[3,8]{1,0:T(4,128)S(1)}, s32[3,8]{1,0:T(4,128)}, u32[]{:S(2)}) copy-start(s32[3,8]{1,0:T(4,128)} %param.8) | copy-start | bytes 292
  7.2 14.9 %copy-start.2 = (s32[256]{0:T(256)S(1)}, s32[256]{0:T(256)}, u32[]{:S(2)}) copy-start(s32[256]{0:T(256)} %param.10) | copy-start | bytes 3076
  7.2 91.7 %all-gather.7.cloned.1.call-start = ((), (), s32[]{:S(2)}) async-start(), calls=%async_computation.1 | async-start | bytes 2113536 | tf_op jit(solution)/shard_map/all_gather | solution.py:25
  7.9 174.0 %all-gather.5.cloned.1.call-start = ((), (), s32[]{:S(2)}) async-start(), calls=%async_computation | async-start | bytes 2113536 | tf_op jit(solution)/shard_map/all_gather | solution.py:24
Sparse Core Ops, SparseCore 0:
  11.1 87.6 all-gather.6
  102.0 79.9 all-gather.4
where the time goes:
time: 1270 us
  blocking collectives  1030 us (81%)
  waiting for transfers between devices  141 us (11%)
  local copies, waits for them, and re-layouts  43.7 us (3%)
  matrix products  37 us (3%)
  between operations  16.2 us (1%)
    psum x1, blocking collectives, body(): proj = lax.psum(proj_terms, 'dev').astype(jnp.bfloat16)  498 us
    psum x1, blocking collectives, body(): gmat = lax.psum(gram_local, 'dev')  491 us
    all_gather x1, waiting for transfers between devices, body(): lax.all_gather(factor_three, 'dev', axis=0, tiled=True)  76.6 us
    all_gather x1, waiting for transfers between devices, body(): lax.all_gather(factor_two, 'dev', axis=0, tiled=True)  62.9 us
    psum x1, blocking collectives, body(): summed = lax.psum(panels, 'grp')  42.2 us
  transfers between devices with their start and end apart: 2, of which 2 were waited for; matrix products, arithmetic and copies ran while one was open for 3% of the time, Pallas kernels for 0%

commit v1 on v0

--- a/solution.py
+++ b/solution.py
@@ -52,7 +52,7 @@
     gram_local = jnp.dot(
         rows.T, rows, precision=lax.Precision.HIGHEST, preferred_element_type=jnp.float32
     )
-    gmat = lax.psum(gram_local, "dev")
+    gmat = jnp.sum(lax.all_gather(gram_local, "dev"), axis=0)
     trace_value = jnp.trace(gmat)
     rows_total = row_blocks * edge * lax.axis_size("dev")
     new_rows = (rows * lax.rsqrt(trace_value / (rows_total * rank_width))).reshape(

time: 1270 us -> 863 us (0.68)
  the two profiles are of different devices: /device:TPU:4 before, /device:TPU:1 now
where the time goes in v1:
time: 863 us; the launch traced here: 862 us
  blocking collectives  536 us (62%)
  waiting for transfers between devices  225 us (26%)
  local copies, waits for them, and re-layouts  43.7 us (5%)
  matrix products  37.7 us (4%)
  between operations  15.9 us (2%)
    psum x1, blocking collectives, body(): proj = lax.psum(proj_terms, 'dev').astype(jnp.bfloat16)  494 us
    all_gather x1, waiting for transfers between devices, body(): gmat = jnp.sum(lax.all_gather(gram_local, 'dev'), axis=0)  82.7 us
    all_gather x1, waiting for transfers between devices, body(): lax.all_gather(factor_three, 'dev', axis=0, tiled=True)  77.8 us
    all_gather x1, waiting for transfers between devices, body(): lax.all_gather(factor_two, 'dev', axis=0, tiled=True)  62.9 us
    psum x1, blocking collectives, body(): summed = lax.psum(panels, 'grp')  42.2 us
  transfers between devices with their start and end apart: 3, of which 3 were waited for; matrix products, arithmetic and copies ran while one was open for 4% of the time, Pallas kernels for 0%

profile of v1, /device:TPU:1, one launch (start us, length us, event | category | flops | bytes accessed | tf_op | source)
XLA Modules:
  0.0 862.0 jit_solution(7118439971676732521)
XLA Ops:
  7.2 0.7 all-gather.11.cloned.1.call-update
  7.9 0.0 all-gather.9.cloned.1.call-start
  7.9 0.7 all-gather.9.cloned.1.call-update
  8.7 0.0 all-gather.7.cloned.1.call-start
  8.7 12.6 %reshape.54 = bf16[8,4096,64]{2,1,0:T(8,128)(2,1)} reshape(bf16[8,64,4096]{2,1,0:T(8,128)(2,1)} %param.7) | data formatting | bytes 8388608 | tf_op jit(solution)/shard_map/reshape | solution.py:35
  22.0 0.1 reshape.58
  22.1 0.2 select_reduce_fusion.3
  22.3 77.8 %all-gather.11.cloned.1.call-done = bf16[128,2,4096]{2,1,0:T(2,128)(2,1)} async-done(((bf16[1,2,4096]{2,1,0:T(2,128)(2,1)}), bf16[128,2,4096]{2,1,0:T(2,128)(2,1)}) %all-gather.11.cloned.1.call-update) | async-done | bytes 2097168 | tf_op jit(solution)/shard_map/all_gather | solution.py:25
  100.1 2.7 reshape.64
  102.8 0.4 convolution_convert_fusion.1
  103.3 0.2 reshape.53
  103.4 8.4 fusion.2
  111.9 8.4 copy.40
  120.2 62.9 %all-gather.9.cloned.1.call-done = bf16[128,2,4096]{2,1,0:T(2,128)(2,1)} async-done(((bf16[1,2,4096]{2,1,0:T(2,128)(2,1)}), bf16[128,2,4096]{2,1,0:T(2,128)(2,1)}) %all-gather.9.cloned.1.call-update) | async-done | bytes 2097168 | tf_op jit(solution)/shard_map/all_gather | solution.py:24
  183.2 2.7 reshape.62
  185.9 0.4 convolution_convert_fusion.2
  186.3 0.2 reshape.52
  186.5 11.5 %convolution_bitcast_fusion = f32[8,64,64,64]{3,2,1,0:T(8,128)} fusion(bf16[8,64,64,64]{3,2,1,0:T(8,128)(2,1)} %bitcast.38, bf16[8,64,64]{2,1,0:T(8,128)(2,1)S(1)} %reshape.52), kind=kOutput, calls=%fused_computation | convolution fusion | flops 268435456 | bytes 12648448 | tf_op jit(solution)/shard_map/bajs,bjr->bars/dot_general | solution.py:40
  198.0 14.8 %reshape.56 = f32[8,64,4096]{2,1,0:T(8,128)} reshape(f32[8,64,64,64]{3,2,1,0:T(8,128)} %convolution_bitcast_fusion) | data formatting | bytes 16777216 | tf_op jit(solution)/shard_map/reshape | solution.py:41
  212.8 15.3 %fusion = f32[2,64,4096]{2,0,1:T(2,128)S(1)} fusion(f32[8,64,4096]{2,1,0:T(8,128)} %reshape.56, f32[8]{0:T(128)S(1)} %compare_convert_fusion, s32[8]{0:T(128)S(1)} %and_select_fusion), kind=kOutput, calls=%fused_computation.1 | convolution fusion | flops 50331680 | bytes 10485824 | tf_op jit(solution)/shard_map/bl,bam->lam/dot_general | solution.py:44
  228.1 1.2 copy.33
  229.3 42.2 %all-reduce.2 = bf16[128,4096]{1,0:T(8,128)(2,1)S(1)} all-reduce(f32[128,4096]{1,0:T(8,128)S(1)} %bitcast.39), channel_id=1, replica_groups=mesh['grp'=4,'dev'=128] {'grp'}, use_global_device_ids=true, to_apply=%region_3.4 | all-reduce | flops 524288 | bytes 3145728 | tf_op jit(solution)/shard_map/psum | solution.py:47
  271.5 0.3 fusion.21
  271.9 493.7 %all-reduce.3 = bf16[4096,64]{0,1:T(8,128)(2,1)S(1)} all-reduce(f32[4096,64]{0,1:T(8,128)S(1)} %fusion.21), channel_id=1, replica_groups=mesh['grp'=4,'dev'=128] {'dev'}, use_global_device_ids=true, to_apply=%region_4.5 | all-reduce | flops 262144 | bytes 1572864 | tf_op jit(solution)/shard_map/psum | solution.py:50
  765.6 0.5 fusion.20
  766.1 0.8 fusion.19
  766.9 82.7 %all-gather.7.cloned.1.call-done = f32[8192,64]{1,0:T(8,128)} async-done(((f32[64,64]{1,0:T(8,128)}), f32[8192,64]{1,0:T(8,128)}) %all-gather.7.cloned.1.call-update) | async-done | bytes 2097168 | tf_op jit(solution)/shard_map/all_gather | solution.py:55
  849.6 2.5 reduce_sum.49
  852.1 0.6 select_reduce_fusion
  853.4 0.6 broadcast_multiply_fusion
  854.7 0.1 copy.34
  854.8 0.7 reshape.59
  (12 shorter events, 0.1 us)
Async XLA Ops:
  7.2 92.9 %all-gather.11.cloned.1.call-start = ((), (), s32[]{:S(2)}) async-start(), calls=%async_computation.2 | async-start | bytes 2113536 | tf_op jit(solution)/shard_map/all_gather | solution.py:25
  7.9 175.3 %all-gather.9.cloned.1.call-start = ((), (), s32[]{:S(2)}) async-start(), calls=%async_computation.1 | async-start | bytes 2113536 | tf_op jit(solution)/shard_map/all_gather | solution.py:24
  8.6 13.3 %copy-start = (bf16[2,4096]{1,0:T(2,128)(2,1)S(1)}, bf16[2,4096]{1,0:T(2,128)(2,1)}, u32[]{:S(2)}) copy-start(bf16[2,4096]{1,0:T(2,128)(2,1)} %param.11) | copy-start | bytes 49156
  8.7 13.4 %copy-start.1 = (s32[3,8]{1,0:T(4,128)S(1)}, s32[3,8]{1,0:T(4,128)}, u32[]{:S(2)}) copy-start(s32[3,8]{1,0:T(4,128)} %param.8) | copy-start | bytes 292
  8.7 13.4 %copy-start.2 = (s32[256]{0:T(256)S(1)}, s32[256]{0:T(256)}, u32[]{:S(2)}) copy-start(s32[256]{0:T(256)} %param.10) | copy-start | bytes 3076
  8.7 840.9 %all-gather.7.cloned.1.call-start = ((), (), s32[]{:S(2)}) async-start(), calls=%async_computation | async-start | bytes 4227072 | tf_op jit(solution)/shard_map/all_gather | solution.py:55
Sparse Core Ops, SparseCore 0:
  11.1 88.9 all-gather.10
  103.2 79.9 all-gather.8
  767.0 82.5 all-gather.6
